TPU v7x, 32 devices: a whole 2x2x4 slice. The times are simulated.
32 devices in a mesh: gx: 8 (over z, y), gy: 4 (over x, core).
Axes of the slice: x: 2, y: 2, z: 4, core: 2. Of those that a mesh axis runs over, the one named last changes fastest.
Arguments:
- layer_in: bfloat16 [8192, 2048], P('gx', 'gy'), may hold values from -15 to 15
- attn_gain: float32 [2048], replicated, may hold values from 0.25 to 1.75
- q_gain: float32 [128], replicated, may hold values from 0.5 to 5
- k_gain: float32 [128], replicated, may hold values from 0.5 to 5
- w_query: bfloat16 [2048, 2048], P('gx', 'gy'), may hold values from -0.125 to 0.125
- w_key: bfloat16 [2048, 1024], P('gx', 'gy'), may hold values from -0.125 to 0.125
- w_value: bfloat16 [2048, 1024], P('gx', 'gy'), may hold values from -0.125 to 0.125
- w_output: bfloat16 [2048, 2048], P('gy', 'gx'), may hold values from -0.375 to 0.375
- mlp_gain: float32 [2048], replicated, may hold values from 0.25 to 1.75
- w_gate: bfloat16 [2048, 6144], P('gx', 'gy'), may hold values from -0.125 to 0.125
- w_up: bfloat16 [2048, 6144], P('gx', 'gy'), may hold values from -0.125 to 0.125
- w_down: bfloat16 [6144, 2048], P('gy', 'gx'), may hold values from -0.078125 to 0.078125
- out_grad: bfloat16 [8192, 2048], P('gx', 'gy'), may hold values from -6 to 6
Outputs:
- layer_out: bfloat16 [8192, 2048], P('gx', 'gy')
- input_grad: float32 [8192, 2048], P('gx', 'gy')
- attn_gain_grad: float32 [2048], replicated
- q_gain_grad: float32 [128], replicated
- k_gain_grad: float32 [128], replicated
- query_grad: float32 [2048, 2048], P('gx', 'gy')
- key_grad: float32 [2048, 1024], P('gx', 'gy')
- value_grad: float32 [2048, 1024], P('gx', 'gy')
- output_grad: float32 [2048, 2048], P('gy', 'gx')
- mlp_gain_grad: float32 [2048], replicated
- gate_grad: float32 [2048, 6144], P('gx', 'gy')
- up_grad: float32 [2048, 6144], P('gx', 'gy')
- down_grad: float32 [6144, 2048], P('gy', 'gx')
All inputs are finite; a program needn't handle non-finite values.
Results may differ from a plain program's by a relative error of at most 0.02.
The roundings to bfloat16 on the way count: a program that leaves them out, or rounds other values in their place, can miss the bound.
Values may be sent and summed in bfloat16 or wider, within the bound.
No kernel may reach another device: no remote copies, remote signals or barrier semaphores. Data moves between devices by JAX's collectives and lax.ppermute only.
A program may use at most 256 MiB of HBM per device.

v0:
```python
import math
import jax
import jax.numpy as jnp
from jax import lax
from jax.sharding import PartitionSpec as P

D = 2048
HQ = 16
HK = 8
HD = 128
L = 512
epsilon = 1e-06
rope_base = 1000000.0


def rope_tables(length, dim_width):
    half_width = dim_width // 2
    frequency = rope_base ** (-(jnp.arange(half_width, dtype=jnp.float32) * (2.0 / dim_width)))
    angles = jnp.arange(length, dtype=jnp.float32)[:, None] * frequency[None, :]
    angles = jnp.concatenate([angles, angles], axis=1)
    return (jnp.cos(angles), jnp.sin(angles))


def rotate(tensor):
    half_width = tensor.shape[-1] // 2
    return jnp.concatenate([-tensor[..., half_width:], tensor[..., :half_width]], axis=-1)


def rotate_back(tensor):
    half_width = tensor.shape[-1] // 2
    return jnp.concatenate([tensor[..., half_width:], -tensor[..., :half_width]], axis=-1)


def head_norm(tensor, gain_vec):
    factor = lax.rsqrt(jnp.mean(tensor * tensor, axis=-1, keepdims=True) + epsilon)
    return (tensor * factor * gain_vec, factor)


def head_norm_back(upstream, tensor, factor, gain_vec):
    weighted = upstream * gain_vec
    return factor * weighted - tensor * factor**3 * jnp.mean(
        weighted * tensor, axis=-1, keepdims=True
    )


def matmul(left, right):
    return jnp.dot(left, right, preferred_element_type=jnp.float32)


def bein(form, left, right):
    return jnp.einsum(form, left, right, preferred_element_type=jnp.float32)


def causal_scores(query_rot, key_rot):
    inv_scale = 1.0 / math.sqrt(HD)
    scores = bein("sihgc,sjhc->shgij", query_rot, key_rot) * inv_scale
    causal = jnp.arange(L)[:, None] >= jnp.arange(L)[None, :]
    return jnp.where(causal, scores, -1e30)


def embed_share(share, column, total_width):
    return lax.dynamic_update_slice(jnp.zeros((total_width,), jnp.float32), share, (column,))


def on_device(
    layer_in,
    attn_gain,
    q_gain,
    k_gain,
    w_query,
    w_key,
    w_value,
    w_output,
    mlp_gain,
    w_gate,
    w_up,
    w_down,
    out_grad,
):
    row_count = layer_in.shape[0]
    part_width = layer_in.shape[1]
    seq_count = row_count // L
    group_size = HQ // HK
    inv_scale = 1.0 / math.sqrt(HD)
    column = lax.axis_index("gy") * part_width
    full_in, grad_full = (
        lax.all_gather(layer_in, "gy", axis=1, tiled=True),
        lax.all_gather(out_grad, "gy", axis=1, tiled=True),
    )
    in_float = full_in.astype(jnp.float32)
    scale_one = lax.rsqrt(jnp.mean(in_float * in_float, axis=1, keepdims=True) + epsilon)
    normed_one = (in_float * scale_one * attn_gain).astype(jnp.bfloat16)
    query_full, key_full, value_full, output_full = (
        lax.all_gather(w_query, "gx", axis=0, tiled=True),
        lax.all_gather(w_key, "gx", axis=0, tiled=True),
        lax.all_gather(w_value, "gx", axis=0, tiled=True),
        lax.all_gather(w_output, "gx", axis=1, tiled=True),
    )
    query_heads = query_full.shape[1] // HD
    key_heads = key_full.shape[1] // HD
    query_act = matmul(normed_one, query_full).reshape(row_count, query_heads, HD)
    key_act = matmul(normed_one, key_full).reshape(row_count, key_heads, HD)
    values = (
        matmul(normed_one, value_full).astype(jnp.bfloat16).reshape(seq_count, L, key_heads, HD)
    )
    query_normed, query_factor = head_norm(query_act, q_gain)
    key_normed, key_factor = head_norm(key_act, k_gain)
    cosine, sine = rope_tables(L, HD)
    cosine = cosine[None, :, None, :]
    sine = sine[None, :, None, :]
    query_seq = query_normed.reshape(seq_count, L, query_heads, HD)
    key_seq = key_normed.reshape(seq_count, L, key_heads, HD)
    query_rot = (
        (query_seq * cosine + rotate(query_seq) * sine)
        .astype(jnp.bfloat16)
        .reshape(seq_count, L, key_heads, group_size, HD)
    )
    key_rot = (key_seq * cosine + rotate(key_seq) * sine).astype(jnp.bfloat16)
    scores = causal_scores(query_rot, key_rot)
    row_top = jnp.max(scores, axis=-1, keepdims=True)
    log_total = row_top + jnp.log(jnp.sum(jnp.exp(scores - row_top), axis=-1, keepdims=True))
    probs = jnp.exp(scores - log_total).astype(jnp.bfloat16)
    attended = bein("shgij,sjhc->sihgc", probs, values).astype(jnp.bfloat16)
    attended_flat = attended.reshape(row_count, query_heads * HD)
    attn_sum = lax.psum(matmul(attended_flat, output_full), "gy")
    mid_float = in_float + attn_sum
    scale_two = lax.rsqrt(jnp.mean(mid_float * mid_float, axis=1, keepdims=True) + epsilon)
    normed_two = (mid_float * scale_two * mlp_gain).astype(jnp.bfloat16)
    gate_full, up_full, down_full = (
        lax.all_gather(w_gate, "gx", axis=0, tiled=True),
        lax.all_gather(w_up, "gx", axis=0, tiled=True),
        lax.all_gather(w_down, "gx", axis=1, tiled=True),
    )
    gate_act = matmul(normed_two, gate_full)
    up_act = matmul(normed_two, up_full)
    sigmoid_gate = jax.nn.sigmoid(gate_act)
    hidden = (gate_act * sigmoid_gate * up_act).astype(jnp.bfloat16)
    mlp_share = lax.psum_scatter(
        matmul(hidden, down_full).astype(jnp.bfloat16), "gy", scatter_dimension=1, tiled=True
    ).astype(jnp.float32)
    mid_share = lax.dynamic_slice_in_dim(mid_float, column, part_width, 1)
    layer_out = (mid_share + mlp_share).astype(jnp.bfloat16)
    grad_hidden = matmul(grad_full, down_full.T)
    down_term = matmul(hidden.T, grad_full)
    grad_gate = (
        grad_hidden * up_act * sigmoid_gate * (1.0 + gate_act * (1.0 - sigmoid_gate))
    ).astype(jnp.bfloat16)
    grad_up = (grad_hidden * gate_act * sigmoid_gate).astype(jnp.bfloat16)
    gate_term = matmul(normed_two.T, grad_gate)
    up_term = matmul(normed_two.T, grad_up)
    grad_two_part = matmul(grad_gate, gate_full.T) + matmul(grad_up, up_full.T)
    grad_two = lax.psum(grad_two_part, "gy")
    mlp_gain_all = jnp.sum(grad_two * mid_float * scale_two, axis=0)
    mlp_gain_own = lax.dynamic_slice_in_dim(mlp_gain_all, column, part_width, 0)
    grad_mid = (
        grad_full.astype(jnp.float32)
        + scale_two * mlp_gain * grad_two
        - mid_float
        * scale_two**3
        * jnp.mean(mlp_gain * grad_two * mid_float, axis=1, keepdims=True)
    )
    grad_mid_bf = grad_mid.astype(jnp.bfloat16)
    grad_mid_share = lax.dynamic_slice_in_dim(grad_mid, column, part_width, 1)
    gate_grad, up_grad, down_grad = (
        lax.psum_scatter(
            gate_term.astype(jnp.bfloat16), "gx", scatter_dimension=0, tiled=True
        ).astype(jnp.float32),
        lax.psum_scatter(
            up_term.astype(jnp.bfloat16), "gx", scatter_dimension=0, tiled=True
        ).astype(jnp.float32),
        lax.psum_scatter(
            down_term.astype(jnp.bfloat16), "gx", scatter_dimension=1, tiled=True
        ).astype(jnp.float32),
    )
    grad_att = matmul(grad_mid_bf, output_full.T).astype(jnp.bfloat16)
    output_term = matmul(attended_flat.T, grad_mid_bf)
    grad_att_seq = grad_att.reshape(seq_count, L, key_heads, group_size, HD)
    probs_again = jnp.exp(causal_scores(query_rot, key_rot) - log_total)
    probs_bf = probs_again.astype(jnp.bfloat16)
    delta = bein("sihgc,sihgc->shgi", grad_att_seq, attended)
    grad_probs = bein("sihgc,sjhc->shgij", grad_att_seq, values)
    grad_scores = (probs_again * (grad_probs - delta[..., None])).astype(jnp.bfloat16)
    grad_qrot = (bein("shgij,sjhc->sihgc", grad_scores, key_rot) * inv_scale).reshape(
        seq_count, L, query_heads, HD
    )
    grad_krot = bein("shgij,sihgc->sjhc", grad_scores, query_rot) * inv_scale
    grad_value_act = bein("shgij,sihgc->sjhc", probs_bf, grad_att_seq)
    grad_qn = (grad_qrot * cosine + rotate_back(grad_qrot * sine)).reshape(
        row_count, query_heads, HD
    )
    grad_kn = (grad_krot * cosine + rotate_back(grad_krot * sine)).reshape(row_count, key_heads, HD)
    q_gain_part = jnp.sum(grad_qn * query_act * query_factor, axis=(0, 1))
    k_gain_part = jnp.sum(grad_kn * key_act * key_factor, axis=(0, 1))
    grad_query = (
        head_norm_back(grad_qn, query_act, query_factor, q_gain)
        .astype(jnp.bfloat16)
        .reshape(row_count, query_heads * HD)
    )
    grad_key = (
        head_norm_back(grad_kn, key_act, key_factor, k_gain)
        .astype(jnp.bfloat16)
        .reshape(row_count, key_heads * HD)
    )
    grad_value = grad_value_act.astype(jnp.bfloat16).reshape(row_count, key_heads * HD)
    query_term = matmul(normed_one.T, grad_query)
    key_term = matmul(normed_one.T, grad_key)
    value_term = matmul(normed_one.T, grad_value)
    grad_one_part = (
        matmul(grad_query, query_full.T)
        + matmul(grad_key, key_full.T)
        + matmul(grad_value, value_full.T)
    )
    grad_one = lax.psum_scatter(
        grad_one_part.astype(jnp.bfloat16), "gy", scatter_dimension=1, tiled=True
    ).astype(jnp.float32)
    query_grad, key_grad, value_grad, output_grad = (
        lax.psum_scatter(
            query_term.astype(jnp.bfloat16), "gx", scatter_dimension=0, tiled=True
        ).astype(jnp.float32),
        lax.psum_scatter(
            key_term.astype(jnp.bfloat16), "gx", scatter_dimension=0, tiled=True
        ).astype(jnp.float32),
        lax.psum_scatter(
            value_term.astype(jnp.bfloat16), "gx", scatter_dimension=0, tiled=True
        ).astype(jnp.float32),
        lax.psum_scatter(
            output_term.astype(jnp.bfloat16), "gx", scatter_dimension=1, tiled=True
        ).astype(jnp.float32),
    )
    in_share = layer_in.astype(jnp.float32)
    gain_share = lax.dynamic_slice_in_dim(attn_gain, column, part_width, 0)
    row_stat = lax.psum(jnp.sum(gain_share * grad_one * in_share, axis=1, keepdims=True), "gy")
    input_grad = (
        grad_mid_share
        + scale_one * gain_share * grad_one
        - in_share * scale_one**3 * (row_stat / D)
    )
    attn_gain_own = jnp.sum(grad_one * in_share * scale_one, axis=0)
    attn_gain_grad, mlp_gain_grad, q_gain_grad, k_gain_grad = lax.psum(
        (
            embed_share(attn_gain_own, column, D),
            embed_share(mlp_gain_own, column, D),
            q_gain_part,
            k_gain_part,
        ),
        ("gx", "gy"),
    )
    return (
        layer_out,
        input_grad,
        attn_gain_grad,
        q_gain_grad,
        k_gain_grad,
        query_grad,
        key_grad,
        value_grad,
        output_grad,
        mlp_gain_grad,
        gate_grad,
        up_grad,
        down_grad,
    )


def solution(mesh):
    placed = (
        P("gx", "gy"),
        P(),
        P(),
        P(),
        P("gx", "gy"),
        P("gx", "gy"),
        P("gx", "gy"),
        P("gy", "gx"),
        P(),
        P("gx", "gy"),
        P("gx", "gy"),
        P("gy", "gx"),
        P("gx", "gy"),
    )
    return jax.shard_map(
        on_device,
        mesh=mesh,
        in_specs=placed,
        out_specs=(
            P("gx", "gy"),
            P("gx", "gy"),
            P(),
            P(),
            P(),
            P("gx", "gy"),
            P("gx", "gy"),
            P("gx", "gy"),
            P("gy", "gx"),
            P(),
            P("gx", "gy"),
            P("gx", "gy"),
            P("gy", "gx"),
        ),
        check_vma=False,
    )
```

profile of v0, /device:TPU:0, one launch (start us, length us, event | category | flops | bytes accessed | tf_op | source)
XLA Modules:
  0.0 1706.3 jit_solution(14412919391294357786)
XLA Ops:
  12.6 34.2 %all-gather.10.cloned.1.call-done = bf16[1024,2048]{1,0:T(8,128)(2,1)} async-done(((bf16[1024,512]{1,0:T(8,128)(2,1)}), bf16[1024,2048]{1,0:T(8,128)(2,1)}) %all-gather.10.cloned.1.call-update) | async-done | bytes 4194320 | tf_op jit(solution)/shard_map/all_gather | solution.py:87
  54.2 43.8 %all-gather.16.cloned.1.call-done = bf16[2048,512]{1,0:T(8,128)(2,1)} async-done(((bf16[256,512]{1,0:T(8,128)(2,1)}), bf16[2048,512]{1,0:T(8,128)(2,1)}) %all-gather.16.cloned.1.call-update) | async-done | bytes 2097168 | tf_op jit(solution)/shard_map/all_gather | solution.py:94
  109.0 30.0 %all-gather.14.cloned.1.call-done = bf16[2048,256]{1,0:T(8,128)(2,1)} async-done(((bf16[256,256]{1,0:T(8,128)(2,1)}), bf16[2048,256]{1,0:T(8,128)(2,1)}) %all-gather.14.cloned.1.call-update) | async-done | bytes 1048592 | tf_op jit(solution)/shard_map/all_gather | solution.py:95
  144.4 35.6 %all-gather.12.cloned.1.call-done = bf16[2048,256]{1,0:T(8,128)(2,1)} async-done(((bf16[256,256]{1,0:T(8,128)(2,1)}), bf16[2048,256]{1,0:T(8,128)(2,1)}) %all-gather.12.cloned.1.call-update) | async-done | bytes 1048592 | tf_op jit(solution)/shard_map/all_gather | solution.py:96
  200.9 30.0 %all-gather.18.cloned.1.call-done = bf16[512,2048]{1,0:T(8,128)(2,1)} async-done(((bf16[512,256]{1,0:T(8,128)(2,1)}), bf16[512,2048]{1,0:T(8,128)(2,1)}) %all-gather.18.cloned.1.call-update) | async-done | bytes 2097168 | tf_op jit(solution)/shard_map/all_gather | solution.py:97
  230.9 7.5 fusion.48
  241.4 148.3 %all-reduce.4.cloned.1.call-done = f32[1024,2048]{1,0:T(8,128)} async-done(((f32[1024,2048]{1,0:T(8,128)}), f32[1024,2048]{1,0:T(8,128)}) %all-reduce.4.cloned.1.call-update) | async-done | bytes 8388624 | tf_op jit(solution)/shard_map/psum | solution.py:125
  401.6 89.2 %all-gather.20.cloned.1.call-done = bf16[2048,1536]{1,0:T(8,128)(2,1)} async-done(((bf16[256,1536]{1,0:T(8,128)(2,1)}), bf16[2048,1536]{1,0:T(8,128)(2,1)}) %all-gather.20.cloned.1.call-update) | async-done | bytes 6291472 | tf_op jit(solution)/shard_map/all_gather | solution.py:130
  490.7 11.7 fusion.49
  502.4 87.4 %all-gather.22.cloned.1.call-done = bf16[2048,1536]{1,0:T(8,128)(2,1)} async-done(((bf16[256,1536]{1,0:T(8,128)(2,1)}), bf16[2048,1536]{1,0:T(8,128)(2,1)}) %all-gather.22.cloned.1.call-update) | async-done | bytes 6291472 | tf_op jit(solution)/shard_map/all_gather | solution.py:131
  589.8 11.8 fusion.50
  601.6 22.5 %all-gather.26.cloned.1.call-done = bf16[1024,2048]{1,0:T(8,128)(2,1)} async-done(((bf16[1024,512]{1,0:T(8,128)(2,1)}), bf16[1024,2048]{1,0:T(8,128)(2,1)}) %all-gather.26.cloned.1.call-update) | async-done | bytes 4194320 | tf_op jit(solution)/shard_map/all_gather | solution.py:88
  624.1 101.4 %all-gather.24.cloned.1.call-done = bf16[1536,2048]{1,0:T(8,128)(2,1)} async-done(((bf16[1536,256]{1,0:T(8,128)(2,1)}), bf16[1536,2048]{1,0:T(8,128)(2,1)}) %all-gather.24.cloned.1.call-update) | async-done | bytes 6291472 | tf_op jit(solution)/shard_map/all_gather | solution.py:132
  725.5 16.4 multiply_convert_fusion.1
  741.9 10.0 fusion.51
  751.9 10.7 convolution_add_fusion
  764.0 149.8 %all-reduce.6.cloned.1.call-done = f32[1024,2048]{1,0:T(8,128)} async-done(((f32[1024,2048]{1,0:T(8,128)}), f32[1024,2048]{1,0:T(8,128)}) %all-reduce.6.cloned.1.call-update) | async-done | bytes 8388624 | tf_op jit(solution)/shard_map/psum | solution.py:152
  913.8 7.2 multiply_reduce_fusion
  977.6 11.0 convolution_convert_fusion.3
  1030.0 7.2 convolution_convert_fusion.4
  1045.1 11.5 convolution_convert_fusion.2
  1056.8 11.5 convolution_convert_fusion.1
  1068.4 11.3 convolution_convert_fusion
  1082.4 11.0 reduce-scatter.16.cloned.1.call-done
  1095.0 44.2 %reduce-scatter.10.cloned.1.call-done = bf16[1024,512]{1,0:T(8,128)(2,1)} async-done(((bf16[1024,2048]{1,0:T(8,128)(2,1)}), bf16[1024,512]{1,0:T(8,128)(2,1)}) %reduce-scatter.10.cloned.1.call-update) | async-done | bytes 1048592 | tf_op jit(solution)/shard_map/reduce_scatter | solution.py:138
  1142.4 69.1 %reduce-scatter.14.cloned.1.call-done = bf16[256,512]{1,0:T(8,128)(2,1)} async-done(((bf16[2048,512]{1,0:T(8,128)(2,1)}), bf16[256,512]{1,0:T(8,128)(2,1)}) %reduce-scatter.14.cloned.1.call-update) | async-done | bytes 262160 | tf_op jit(solution)/shard_map/reduce_scatter | solution.py:217
  1213.3 69.6 %reduce-scatter.20.cloned.1.call-done = bf16[512,256]{1,0:T(8,128)(2,1)} async-done(((bf16[512,2048]{1,0:T(8,128)(2,1)}), bf16[512,256]{1,0:T(8,128)(2,1)}) %reduce-scatter.20.cloned.1.call-update) | async-done | bytes 262160 | tf_op jit(solution)/shard_map/reduce_scatter | solution.py:226
  1284.7 43.9 %reduce-scatter.12.cloned.1.call-done = bf16[1024,512]{1,0:T(8,128)(2,1)} async-done(((bf16[1024,2048]{1,0:T(8,128)(2,1)}), bf16[1024,512]{1,0:T(8,128)(2,1)}) %reduce-scatter.12.cloned.1.call-update) | async-done | bytes 1048592 | tf_op jit(solution)/shard_map/reduce_scatter | solution.py:213
  1331.2 118.9 %reduce-scatter.22.cloned.1.call-done = bf16[256,1536]{1,0:T(8,128)(2,1)} async-done(((bf16[2048,1536]{1,0:T(8,128)(2,1)}), bf16[256,1536]{1,0:T(8,128)(2,1)}) %reduce-scatter.22.cloned.1.call-update) | async-done | bytes 786448 | tf_op jit(solution)/shard_map/reduce_scatter | solution.py:165
  1452.6 118.4 %reduce-scatter.24.cloned.1.call-done = bf16[256,1536]{1,0:T(8,128)(2,1)} async-done(((bf16[2048,1536]{1,0:T(8,128)(2,1)}), bf16[256,1536]{1,0:T(8,128)(2,1)}) %reduce-scatter.24.cloned.1.call-update) | async-done | bytes 786448 | tf_op jit(solution)/shard_map/reduce_scatter | solution.py:168
  1573.5 43.1 %all-reduce = (f32[2048]{0:T(1024)}, f32[128]{0:T(128)}, f32[128]{0:T(128)}, f32[2048]{0:T(1024)}) all-reduce(f32[2048]{0:T(1024)S(1)} %dynamic_update_slice.6, f32[128]{0:T(128)S(1)} %bitcast_reduce_fusion, f32[128]{0:T(128)S(1)} %get-tuple-element.21, ...), channel_id=1, replica_groups=mesh['gx'=8,'gy'=4] {'gx','gy'}, use_global_device_ids=true, to_apply=%region_16.17 | all-reduce | flops 4352 | bytes 34816 | tf_op jit(solution)/shard_map/psum | solution.py:239
  1623.1 70.1 %reduce-scatter.26.cloned.1.call-done = bf16[1536,256]{1,0:T(8,128)(2,1)} async-done(((bf16[1536,2048]{1,0:T(8,128)(2,1)}), bf16[1536,256]{1,0:T(8,128)(2,1)}) %reduce-scatter.26.cloned.1.call-update) | async-done | bytes 786448 | tf_op jit(solution)/shard_map/reduce_scatter | solution.py:171
  (249 shorter events, 202.7 us)
Async XLA Ops:
  7.2 44.0 %copy-start.48 = (f32[2048]{0:T(1024)S(1)}, f32[2048]{0:T(1024)}, u32[]{:S(2)}) copy-start(f32[2048]{0:T(1024)} %param.14) | copy-start | bytes 24580
  7.2 39.6 %all-gather.10.cloned.1.call-start = ((), (), s32[]{:S(2)}) async-start(), calls=%async_computation.9 | async-start | bytes 5242880 | tf_op jit(solution)/shard_map/all_gather | solution.py:87
  7.9 90.1 %all-gather.16.cloned.1.call-start = ((), (), s32[]{:S(2)}) async-start(), calls=%async_computation.12 | async-start | bytes 2359296 | tf_op jit(solution)/shard_map/all_gather | solution.py:94
  8.7 130.3 %all-gather.14.cloned.1.call-start = ((), (), s32[]{:S(2)}) async-start(), calls=%async_computation.11 | async-start | bytes 1179648 | tf_op jit(solution)/shard_map/all_gather | solution.py:95
  9.4 170.6 %all-gather.12.cloned.1.call-start = ((), (), s32[]{:S(2)}) async-start(), calls=%async_computation.10 | async-start | bytes 1179648 | tf_op jit(solution)/shard_map/all_gather | solution.py:96
  10.0 221.0 %all-gather.18.cloned.1.call-start = ((), (), s32[]{:S(2)}) async-start(), calls=%async_computation.13 | async-start | bytes 2359296 | tf_op jit(solution)/shard_map/all_gather | solution.py:97
  10.6 379.1 %all-reduce.4.cloned.1.call-start = ((), (), s32[]{:S(2)}) async-start(), calls=%async_computation.14 | async-start | bytes 16777216 | tf_op jit(solution)/shard_map/psum | solution.py:125
  144.3 41.8 %copy-start.41 = (f32[1024,4]{0,1:T(4,128)}, f32[1024,4]{0,1:T(4,128)S(1)}, u32[]{:S(2)}) copy-start(f32[1024,4]{0,1:T(4,128)S(1)} %get-tuple-element.45) | copy-start | bytes 49156
  144.4 40.3 %copy-start.51 = (f32[128]{0:T(128)S(1)}, f32[128]{0:T(128)}, u32[]{:S(2)}) copy-start(f32[128]{0:T(128)} %param.16) | copy-start | bytes 1540
  196.2 42.3 %copy-start.19 = (bf16[2,2,128,2,512]{4,2,3,1,0:T(8,128)(2,1)}, bf16[2,2,128,2,512]{4,2,3,1,0:T(8,128)(2,1)S(1)}, u32[]{:S(2)}) copy-start(bf16[2,2,128,2,512]{4,2,3,1,0:T(8,128)(2,1)S(1)} %convolution_convert_fusion.8) | copy-start | bytes 3145732
  238.5 252.3 %all-gather.20.cloned.1.call-start = ((), (), s32[]{:S(2)}) async-start(), calls=%async_computation.15 | async-start | bytes 7077888 | tf_op jit(solution)/shard_map/all_gather | solution.py:130
  239.2 350.6 %all-gather.22.cloned.1.call-start = ((), (), s32[]{:S(2)}) async-start(), calls=%async_computation.16 | async-start | bytes 7077888 | tf_op jit(solution)/shard_map/all_gather | solution.py:131
  240.0 384.1 %all-gather.26.cloned.1.call-start = ((), (), s32[]{:S(2)}) async-start(), calls=%async_computation.19 | async-start | bytes 5242880 | tf_op jit(solution)/shard_map/all_gather | solution.py:88
  240.7 484.8 %all-gather.24.cloned.1.call-start = ((), (), s32[]{:S(2)}) async-start(), calls=%async_computation.17 | async-start | bytes 7077888 | tf_op jit(solution)/shard_map/all_gather | solution.py:132
  241.3 157.4 %copy-start.43 = (f32[2048]{0:T(1024)S(1)}, f32[2048]{0:T(1024)}, u32[]{:S(2)}) copy-start(f32[2048]{0:T(1024)} %param.21) | copy-start | bytes 24580
  241.3 672.5 %all-reduce.6.cloned.1.call-start = ((), (), s32[]{:S(2)}) async-start(), calls=%async_computation.20 | async-start | bytes 16777216 | tf_op jit(solution)/shard_map/psum | solution.py:152
  741.9 10.0 copy-start.54
  741.9 10.0 copy-start.52
  762.6 318.1 %reduce-scatter.18.cloned.1.call-start = ((), (), s32[]{:S(2)}) async-start(), calls=%async_computation.24 | async-start | bytes 1179648 | tf_op jit(solution)/shard_map/reduce_scatter | solution.py:223
  913.8 9.4 copy-start.18
  961.6 131.8 %reduce-scatter.16.cloned.1.call-start = ((), (), s32[]{:S(2)}) async-start(), calls=%async_computation.23 | async-start | bytes 1179648 | tf_op jit(solution)/shard_map/reduce_scatter | solution.py:220
  977.5 161.7 %reduce-scatter.10.cloned.1.call-start = ((), (), s32[]{:S(2)}) async-start(), calls=%async_computation.18 | async-start | bytes 5242880 | tf_op jit(solution)/shard_map/reduce_scatter | solution.py:138
  988.6 222.9 %reduce-scatter.14.cloned.1.call-start = ((), (), s32[]{:S(2)}) async-start(), calls=%async_computation.22 | async-start | bytes 2359296 | tf_op jit(solution)/shard_map/reduce_scatter | solution.py:217
  1029.9 253.0 %reduce-scatter.20.cloned.1.call-start = ((), (), s32[]{:S(2)}) async-start(), calls=%async_computation.25 | async-start | bytes 2359296 | tf_op jit(solution)/shard_map/reduce_scatter | solution.py:226
  1037.3 291.4 %reduce-scatter.12.cloned.1.call-start = ((), (), s32[]{:S(2)}) async-start(), calls=%async_computation.21 | async-start | bytes 5242880 | tf_op jit(solution)/shard_map/reduce_scatter | solution.py:213
  1045.0 405.1 %reduce-scatter.22.cloned.1.call-start = ((), (), s32[]{:S(2)}) async-start(), calls=%async_computation.26 | async-start | bytes 7077888 | tf_op jit(solution)/shard_map/reduce_scatter | solution.py:165
  1056.6 514.5 %reduce-scatter.24.cloned.1.call-start = ((), (), s32[]{:S(2)}) async-start(), calls=%async_computation.27 | async-start | bytes 7077888 | tf_op jit(solution)/shard_map/reduce_scatter | solution.py:168
  1068.3 625.0 %reduce-scatter.26.cloned.1.call-start = ((), (), s32[]{:S(2)}) async-start(), calls=%async_computation.28 | async-start | bytes 7077888 | tf_op jit(solution)/shard_map/reduce_scatter | solution.py:171
  1079.7 249.0 %copy-start.9 = (bf16[1024,512]{1,0:T(8,128)(2,1)S(1)}, bf16[1024,512]{1,0:T(8,128)(2,1)}, u32[]{:S(2)}) copy-start(bf16[1024,512]{1,0:T(8,128)(2,1)} %param.13) | copy-start | bytes 3145732
  1079.7 249.0 %copy-start.46 = (f32[1024]{0:T(1024)S(1)}, f32[1024]{0:T(1024)}, u32[]{:S(2)}) copy-start(f32[1024]{0:T(1024)} %copy-done.45) | copy-start | bytes 12292
  1284.7 411.0 %copy-start.47 = (f32[1024]{0:T(1024)S(1)}, f32[1024]{0:T(1024)}, u32[]{:S(2)}) copy-start(f32[1024]{0:T(1024)} %get-tuple-element.48) | copy-start | bytes 12292
  1328.7 367.0 %copy-start.25 = (bf16[1024,512]{1,0:T(8,128)(2,1)S(1)}, bf16[1024,512]{1,0:T(8,128)(2,1)}, u32[]{:S(2)}) copy-start(bf16[1024,512]{1,0:T(8,128)(2,1)} %reduce-scatter.12.cloned.1.call-done) | copy-start | bytes 3145732
  (44 other events, 147.6 us)
Sparse Core Ops, SparseCore 0:
  9.6 37.1 all-gather.9
  48.9 49.0 all-gather.15
  100.1 38.7 all-gather.13
  141.0 38.9 all-gather.11
  181.9 49.0 all-gather.17
  238.6 151.0 all-reduce.3
  391.9 98.8 all-gather.19
  492.9 96.8 all-gather.21
  591.4 32.6 all-gather.25
  626.0 99.4 all-gather.23
  762.8 151.0 all-reduce.5
  961.7 64.4 reduce-scatter.17
  1030.2 63.1 reduce-scatter.15
  1095.7 43.3 reduce-scatter.9
  1143.1 68.3 reduce-scatter.13
  1214.9 67.9 reduce-scatter.19
  1285.3 43.2 reduce-scatter.11
  1332.1 118.0 reduce-scatter.21
  1453.7 117.2 reduce-scatter.23
  1574.5 118.7 reduce-scatter.25
where the time goes:
time: 1710 us
  waiting for transfers between devices  1320 us (77%)
  matrix products  179 us (10%)
  other arithmetic  71 us (4%)
  local copies, waits for them, and re-layouts  65.8 us (4%)
  blocking collectives  49.6 us (3%)
    dot_general x21, matrix products, matmul(): return jnp.dot(left, right, preferred_element_type=jnp.float32)  156 us
    psum x1, waiting for transfers between devices, on_device(): grad_two = lax.psum(grad_two_part, 'gy')  150 us
    psum x1, waiting for transfers between devices, on_device(): attn_sum = lax.psum(matmul(attended_flat, output_full), 'gy')  148 us
    reduce_scatter x1, waiting for transfers between devices, on_device(): lax.psum_scatter(gate_term.astype(jnp.bfloat16), 'gx', scatter_dimension=...  119 us
    reduce_scatter x1, waiting for transfers between devices, on_device(): lax.psum_scatter(up_term.astype(jnp.bfloat16), 'gx', scatter_dimension=0,...  118 us
    all_gather x1, waiting for transfers between devices, on_device(): lax.all_gather(w_down, 'gx', axis=1, tiled=True)  101 us
    all_gather x1, waiting for transfers between devices, on_device(): lax.all_gather(w_gate, 'gx', axis=0, tiled=True)  89.2 us
    all_gather x1, waiting for transfers between devices, on_device(): lax.all_gather(w_up, 'gx', axis=0, tiled=True)  87.4 us
  transfers between devices with their start and end apart: 20, of which 19 were waited for; matrix products, arithmetic and copies ran while one was open for 12% of the time, Pallas kernels for 0%

commit v1 on v0

--- a/solution.py
+++ b/solution.py
@@ -11,6 +11,22 @@
 L = 512
 epsilon = 1e-06
 rope_base = 1000000.0
+
+
+def collect(x, axis, dim):
+    ways, here, lap = (lax.axis_size(axis), lax.axis_index(axis), x.shape[dim])
+    lengths = [n * ways if d == dim else n for d, n in enumerate(x.shape)]
+    full = lax.dynamic_update_slice_in_dim(jnp.zeros(lengths, x.dtype), x, here * lap, axis=dim)
+    going_up = going_down = x
+    for far in range(1, ways // 2 + 1):
+        going_up = lax.ppermute(going_up, axis, [(d, (d + 1) % ways) for d in range(ways)])
+        full = lax.dynamic_update_slice_in_dim(full, going_up, (here - far) % ways * lap, axis=dim)
+        if 2 * far < ways:
+            going_down = lax.ppermute(going_down, axis, [(d, (d - 1) % ways) for d in range(ways)])
+            full = lax.dynamic_update_slice_in_dim(
+                full, going_down, (here + far) % ways * lap, axis=dim
+            )
+    return full
 
 
 def rope_tables(length, dim_width):
@@ -127,7 +143,7 @@
     scale_two = lax.rsqrt(jnp.mean(mid_float * mid_float, axis=1, keepdims=True) + epsilon)
     normed_two = (mid_float * scale_two * mlp_gain).astype(jnp.bfloat16)
     gate_full, up_full, down_full = (
-        lax.all_gather(w_gate, "gx", axis=0, tiled=True),
+        collect(w_gate, "gx", 0),
         lax.all_gather(w_up, "gx", axis=0, tiled=True),
         lax.all_gather(w_down, "gx", axis=1, tiled=True),
     )

time: 1710 us -> 1620 us (0.947)
  waiting for transfers between devices: 1320 us -> 1180 us
  starting transfers between devices: 1.8 us -> 43.7 us
    psum x1, waiting for transfers between devices: 148 us -> 22.3 us  [on_device(): attn_sum = lax.psum(matmul(attended_flat, output_full), 'gy')]
    all_gather x1 -> x0, waiting for transfers between devices: 89.2 us -> none  [on_device(): lax.all_gather(w_gate, 'gx', axis=0, tiled=True)]
    ppermute x0 -> x7, waiting for transfers between devices: none -> 69.4 us  [the longest x4 69.4 us: collect(): lax.ppermute(going_up, axis, [(d, (d + 1) % ways) for d in range(ways)])]
    ppermute x0 -> x7, starting transfers between devices: none -> 41.9 us  [the longest x3 32.8 us: collect(): lax.ppermute(going_down, axis, [(d, (d - 1) % ways) for d in range(ways)])]
  transfers between devices with their start and end apart: 20 -> 26, of which waited for: 19 -> 22; matrix products, arithmetic and copies ran while one was open for 12% -> 13% of each run, Pallas kernels for 0% -> 0%
where the time goes in v1:
time: 1620 us
  waiting for transfers between devices  1180 us (73%)
  matrix products  177 us (11%)
  local copies, waits for them, and re-layouts  81.4 us (5%)
  other arithmetic  71.8 us (4%)
  blocking collectives  49.6 us (3%)
  starting transfers between devices  43.7 us (3%)
    dot_general x21, matrix products, matmul(): return jnp.dot(left, right, preferred_element_type=jnp.float32)  154 us
    psum x1, waiting for transfers between devices, on_device(): grad_two = lax.psum(grad_two_part, 'gy')  150 us
    reduce_scatter x1, waiting for transfers between devices, on_device(): lax.psum_scatter(gate_term.astype(jnp.bfloat16), 'gx', scatter_dimension=...  119 us
    reduce_scatter x1, waiting for transfers between devices, on_device(): lax.psum_scatter(up_term.astype(jnp.bfloat16), 'gx', scatter_dimension=0,...  118 us
    all_gather x1, waiting for transfers between devices, on_device(): lax.all_gather(w_down, 'gx', axis=1, tiled=True)  102 us
    all_gather x1, waiting for transfers between devices, on_device(): lax.all_gather(w_up, 'gx', axis=0, tiled=True)  89.3 us
    reduce_scatter x1, waiting for transfers between devices, on_device(): lax.psum_scatter(down_term.astype(jnp.bfloat16), 'gx', scatter_dimension=...  70.3 us
    reduce_scatter x1, waiting for transfers between devices, on_device(): lax.psum_scatter(query_term.astype(jnp.bfloat16), 'gx', scatter_dimension...  69.6 us
  transfers between devices with their start and end apart: 26, of which 22 were waited for; matrix products, arithmetic and copies ran while one was open for 13% of the time, Pallas kernels for 0%

profile of v1, /device:TPU:0, one launch (start us, length us, event | category | flops | bytes accessed | tf_op | source)
XLA Modules:
  0.0 1616.5 jit_solution(7528630260785945360)
XLA Ops:
  12.6 34.2 %all-gather.9.cloned.1.call-done = bf16[1024,2048]{1,0:T(8,128)(2,1)} async-done(((bf16[1024,512]{1,0:T(8,128)(2,1)}), bf16[1024,2048]{1,0:T(8,128)(2,1)}) %all-gather.9.cloned.1.call-update) | async-done | bytes 4194320 | tf_op jit(solution)/shard_map/all_gather | solution.py:103
  54.3 43.7 %all-gather.15.cloned.1.call-done = bf16[2048,512]{1,0:T(8,128)(2,1)} async-done(((bf16[256,512]{1,0:T(8,128)(2,1)}), bf16[2048,512]{1,0:T(8,128)(2,1)}) %all-gather.15.cloned.1.call-update) | async-done | bytes 2097168 | tf_op jit(solution)/shard_map/all_gather | solution.py:110
  109.1 29.9 %all-gather.13.cloned.1.call-done = bf16[2048,256]{1,0:T(8,128)(2,1)} async-done(((bf16[256,256]{1,0:T(8,128)(2,1)}), bf16[2048,256]{1,0:T(8,128)(2,1)}) %all-gather.13.cloned.1.call-update) | async-done | bytes 1048592 | tf_op jit(solution)/shard_map/all_gather | solution.py:111
  145.0 35.0 %all-gather.11.cloned.1.call-done = bf16[2048,256]{1,0:T(8,128)(2,1)} async-done(((bf16[256,256]{1,0:T(8,128)(2,1)}), bf16[2048,256]{1,0:T(8,128)(2,1)}) %all-gather.11.cloned.1.call-update) | async-done | bytes 1048592 | tf_op jit(solution)/shard_map/all_gather | solution.py:112
  200.9 30.1 %all-gather.17.cloned.1.call-done = bf16[512,2048]{1,0:T(8,128)(2,1)} async-done(((bf16[512,256]{1,0:T(8,128)(2,1)}), bf16[512,2048]{1,0:T(8,128)(2,1)}) %all-gather.17.cloned.1.call-update) | async-done | bytes 2097168 | tf_op jit(solution)/shard_map/all_gather | solution.py:113
  245.6 30.5 %collective-permute-done = bf16[256,1536]{1,0:T(8,128)(2,1)S(1)} collective-permute-done((bf16[256,1536]{1,0:T(8,128)(2,1)S(1)}, bf16[256,1536]{1,0:T(8,128)(2,1)S(1)}, u32[]{:S(2)}, u32[]{:S(2)}) %collective-permute-start) | collective-permute-done | bytes 786464 | tf_op jit(solution)/shard_map/ppermute | solution.py:22
  278.6 16.7 %collective-permute-start.3 = (bf16[256,1536]{1,0:T(8,128)(2,1)}, bf16[256,1536]{1,0:T(8,128)(2,1)}, u32[]{:S(2)}, u32[]{:S(2)}) collective-permute-start(bf16[256,1536]{1,0:T(8,128)(2,1)} %collective-permute-done.1), channel_id=1, source_target_pairs={{0,28},{4,0},{8,4},{12,8},{16,12},{20,16},{24,20},{28,24},{1,29},{... | collective-permute-start | bytes 2359304 | tf_op jit(solution)/shard_map/ppermute | solution.py:25
  295.3 16.3 %collective-permute-done.2 = bf16[256,1536]{1,0:T(8,128)(2,1)} collective-permute-done((bf16[256,1536]{1,0:T(8,128)(2,1)S(1)}, bf16[256,1536]{1,0:T(8,128)(2,1)}, u32[]{:S(2)}, u32[]{:S(2)}) %collective-permute-start.2) | collective-permute-done | bytes 786464 | tf_op jit(solution)/shard_map/ppermute | solution.py:22
  319.2 12.9 collective-permute-start.5
  334.1 12.6 collective-permute-done.4
  367.5 22.3 %all-reduce.4.cloned.1.call-done = f32[1024,2048]{1,0:T(8,128)} async-done(((f32[1024,2048]{1,0:T(8,128)}), f32[1024,2048]{1,0:T(8,128)}) %all-reduce.4.cloned.1.call-update) | async-done | bytes 8388624 | tf_op jit(solution)/shard_map/psum | solution.py:141
  401.5 89.3 %all-gather.19.cloned.1.call-done = bf16[2048,1536]{1,0:T(8,128)(2,1)} async-done(((bf16[256,1536]{1,0:T(8,128)(2,1)}), bf16[2048,1536]{1,0:T(8,128)(2,1)}) %all-gather.19.cloned.1.call-update) | async-done | bytes 6291472 | tf_op jit(solution)/shard_map/all_gather | solution.py:147
  490.8 11.7 fusion.49
  502.5 22.5 %all-gather.23.cloned.1.call-done = bf16[1024,2048]{1,0:T(8,128)(2,1)} async-done(((bf16[1024,512]{1,0:T(8,128)(2,1)}), bf16[1024,2048]{1,0:T(8,128)(2,1)}) %all-gather.23.cloned.1.call-update) | async-done | bytes 4194320 | tf_op jit(solution)/shard_map/all_gather | solution.py:104
  525.1 101.6 %all-gather.21.cloned.1.call-done = bf16[1536,2048]{1,0:T(8,128)(2,1)} async-done(((bf16[1536,256]{1,0:T(8,128)(2,1)}), bf16[1536,2048]{1,0:T(8,128)(2,1)}) %all-gather.21.cloned.1.call-update) | async-done | bytes 6291472 | tf_op jit(solution)/shard_map/all_gather | solution.py:148
  626.6 11.9 fusion.50
  638.5 15.9 multiply_convert_fusion.2
  661.1 11.9 convolution_add_fusion
  674.4 149.8 %all-reduce.6.cloned.1.call-done = f32[1024,2048]{1,0:T(8,128)} async-done(((f32[1024,2048]{1,0:T(8,128)}), f32[1024,2048]{1,0:T(8,128)}) %all-reduce.6.cloned.1.call-update) | async-done | bytes 8388624 | tf_op jit(solution)/shard_map/psum | solution.py:168
  888.0 11.0 convolution_convert_fusion.3
  955.8 11.5 convolution_convert_fusion.2
  967.7 11.5 convolution_convert_fusion.1
  979.3 11.3 convolution_convert_fusion
  993.3 10.2 reduce-scatter.16.cloned.1.call-done
  1005.1 44.4 %reduce-scatter.10.cloned.1.call-done = bf16[1024,512]{1,0:T(8,128)(2,1)} async-done(((bf16[1024,2048]{1,0:T(8,128)(2,1)}), bf16[1024,512]{1,0:T(8,128)(2,1)}) %reduce-scatter.10.cloned.1.call-update) | async-done | bytes 1048592 | tf_op jit(solution)/shard_map/reduce_scatter | solution.py:154
  1052.7 69.1 %reduce-scatter.20.cloned.1.call-done = bf16[512,256]{1,0:T(8,128)(2,1)} async-done(((bf16[512,2048]{1,0:T(8,128)(2,1)}), bf16[512,256]{1,0:T(8,128)(2,1)}) %reduce-scatter.20.cloned.1.call-update) | async-done | bytes 262160 | tf_op jit(solution)/shard_map/reduce_scatter | solution.py:242
  1123.6 69.6 %reduce-scatter.14.cloned.1.call-done = bf16[256,512]{1,0:T(8,128)(2,1)} async-done(((bf16[2048,512]{1,0:T(8,128)(2,1)}), bf16[256,512]{1,0:T(8,128)(2,1)}) %reduce-scatter.14.cloned.1.call-update) | async-done | bytes 262160 | tf_op jit(solution)/shard_map/reduce_scatter | solution.py:233
  1195.1 44.0 %reduce-scatter.12.cloned.1.call-done = bf16[1024,512]{1,0:T(8,128)(2,1)} async-done(((bf16[1024,2048]{1,0:T(8,128)(2,1)}), bf16[1024,512]{1,0:T(8,128)(2,1)}) %reduce-scatter.12.cloned.1.call-update) | async-done | bytes 1048592 | tf_op jit(solution)/shard_map/reduce_scatter | solution.py:229
  1241.6 118.9 %reduce-scatter.22.cloned.1.call-done = bf16[256,1536]{1,0:T(8,128)(2,1)} async-done(((bf16[2048,1536]{1,0:T(8,128)(2,1)}), bf16[256,1536]{1,0:T(8,128)(2,1)}) %reduce-scatter.22.cloned.1.call-update) | async-done | bytes 786448 | tf_op jit(solution)/shard_map/reduce_scatter | solution.py:181
  1362.9 118.3 %reduce-scatter.24.cloned.1.call-done = bf16[256,1536]{1,0:T(8,128)(2,1)} async-done(((bf16[2048,1536]{1,0:T(8,128)(2,1)}), bf16[256,1536]{1,0:T(8,128)(2,1)}) %reduce-scatter.24.cloned.1.call-update) | async-done | bytes 786448 | tf_op jit(solution)/shard_map/reduce_scatter | solution.py:184
  1483.7 43.2 %all-reduce = (f32[2048]{0:T(1024)}, f32[128]{0:T(128)}, f32[128]{0:T(128)}, f32[2048]{0:T(1024)}) all-reduce(f32[2048]{0:T(1024)S(1)} %dynamic_update_slice.38, f32[128]{0:T(128)S(1)} %bitcast_reduce_fusion, f32[128]{0:T(128)S(1)} %get-tuple-element.21, ...), channel_id=1, replica_groups=mesh['gx'=8,'gy'=4] {'gx','gy'}, use_global_device_ids=true, to_apply=%region_16.17 | all-reduce | flops 4352 | bytes 34816 | tf_op jit(solution)/shard_map/psum | solution.py:255
  1533.3 70.3 %reduce-scatter.26.cloned.1.call-done = bf16[1536,256]{1,0:T(8,128)(2,1)} async-done(((bf16[1536,2048]{1,0:T(8,128)(2,1)}), bf16[1536,256]{1,0:T(8,128)(2,1)}) %reduce-scatter.26.cloned.1.call-update) | async-done | bytes 786448 | tf_op jit(solution)/shard_map/reduce_scatter | solution.py:187
  (282 shorter events, 269.3 us)
Async XLA Ops:
  7.2 44.0 %copy-start.53 = (f32[2048]{0:T(1024)S(1)}, f32[2048]{0:T(1024)}, u32[]{:S(2)}) copy-start(f32[2048]{0:T(1024)} %param.14) | copy-start | bytes 24580
  7.2 39.6 %all-gather.9.cloned.1.call-start = ((), (), s32[]{:S(2)}) async-start(), calls=%async_computation.9 | async-start | bytes 5242880 | tf_op jit(solution)/shard_map/all_gather | solution.py:103
  7.9 90.1 %all-gather.15.cloned.1.call-start = ((), (), s32[]{:S(2)}) async-start(), calls=%async_computation.12 | async-start | bytes 2359296 | tf_op jit(solution)/shard_map/all_gather | solution.py:110
  8.7 130.3 %all-gather.13.cloned.1.call-start = ((), (), s32[]{:S(2)}) async-start(), calls=%async_computation.11 | async-start | bytes 1179648 | tf_op jit(solution)/shard_map/all_gather | solution.py:111
  9.4 170.6 %all-gather.11.cloned.1.call-start = ((), (), s32[]{:S(2)}) async-start(), calls=%async_computation.10 | async-start | bytes 1179648 | tf_op jit(solution)/shard_map/all_gather | solution.py:112
  10.0 221.0 %all-gather.17.cloned.1.call-start = ((), (), s32[]{:S(2)}) async-start(), calls=%async_computation.13 | async-start | bytes 2359296 | tf_op jit(solution)/shard_map/all_gather | solution.py:113
  10.6 379.2 %all-reduce.4.cloned.1.call-start = ((), (), s32[]{:S(2)}) async-start(), calls=%async_computation.14 | async-start | bytes 16777216 | tf_op jit(solution)/shard_map/psum | solution.py:141
  196.1 42.4 %copy-start.20 = (bf16[2,2,128,2,512]{4,2,3,1,0:T(8,128)(2,1)}, bf16[2,2,128,2,512]{4,2,3,1,0:T(8,128)(2,1)S(1)}, u32[]{:S(2)}) copy-start(bf16[2,2,128,2,512]{4,2,3,1,0:T(8,128)(2,1)S(1)} %convolution_convert_fusion.8) | copy-start | bytes 3145732
  238.6 252.3 %all-gather.19.cloned.1.call-start = ((), (), s32[]{:S(2)}) async-start(), calls=%async_computation.15 | async-start | bytes 7077888 | tf_op jit(solution)/shard_map/all_gather | solution.py:147
  239.3 285.7 %all-gather.23.cloned.1.call-start = ((), (), s32[]{:S(2)}) async-start(), calls=%async_computation.18 | async-start | bytes 5242880 | tf_op jit(solution)/shard_map/all_gather | solution.py:104
  240.1 386.6 %all-gather.21.cloned.1.call-start = ((), (), s32[]{:S(2)}) async-start(), calls=%async_computation.16 | async-start | bytes 7077888 | tf_op jit(solution)/shard_map/all_gather | solution.py:148
  240.8 583.4 %all-reduce.6.cloned.1.call-start = ((), (), s32[]{:S(2)}) async-start(), calls=%async_computation.19 | async-start | bytes 16777216 | tf_op jit(solution)/shard_map/psum | solution.py:168
  240.9 35.3 %collective-permute-start = (bf16[256,1536]{1,0:T(8,128)(2,1)S(1)}, bf16[256,1536]{1,0:T(8,128)(2,1)S(1)}, u32[]{:S(2)}, u32[]{:S(2)}) collective-permute-start(bf16[256,1536]{1,0:T(8,128)(2,1)S(1)} %copy-done.41), channel_id=1, source_target_pairs={{0,4},{4,8},{8,12},{12,16},{16,20},{20,24},{24,28},{28,0},{1,5},{5... | collective-permute-start | bytes 2359304 | tf_op jit(solution)/shard_map/ppermute | solution.py:22
  242.4 36.2 %collective-permute-start.1 = (bf16[256,1536]{1,0:T(8,128)(2,1)S(1)}, bf16[256,1536]{1,0:T(8,128)(2,1)}, u32[]{:S(2)}, u32[]{:S(2)}) collective-permute-start(bf16[256,1536]{1,0:T(8,128)(2,1)S(1)} %copy-done.41), channel_id=1, source_target_pairs={{0,28},{4,0},{8,4},{12,8},{16,12},{20,16},{24,20},{28,24},{1,29},{... | collective-permute-start | bytes 2359304 | tf_op jit(solution)/shard_map/ppermute | solution.py:25
  276.1 35.5 %collective-permute-start.2 = (bf16[256,1536]{1,0:T(8,128)(2,1)S(1)}, bf16[256,1536]{1,0:T(8,128)(2,1)}, u32[]{:S(2)}, u32[]{:S(2)}) collective-permute-start(bf16[256,1536]{1,0:T(8,128)(2,1)S(1)} %collective-permute-done), channel_id=1, source_target_pairs={{0,4},{4,8},{8,12},{12,16},{16,20},{20,24},{24,28},{28,0},{1,5},{5... | collective-permute-start | bytes 2359304 | tf_op jit(solution)/shard_map/ppermute | solution.py:22
  278.6 40.5 %collective-permute-start.3 = (bf16[256,1536]{1,0:T(8,128)(2,1)}, bf16[256,1536]{1,0:T(8,128)(2,1)}, u32[]{:S(2)}, u32[]{:S(2)}) collective-permute-start(bf16[256,1536]{1,0:T(8,128)(2,1)} %collective-permute-done.1), channel_id=1, source_target_pairs={{0,28},{4,0},{8,4},{12,8},{16,12},{20,16},{24,20},{28,24},{1,29},{... | collective-permute-start | bytes 2359304 | tf_op jit(solution)/shard_map/ppermute | solution.py:25
  311.6 35.1 %collective-permute-start.4 = (bf16[256,1536]{1,0:T(8,128)(2,1)}, bf16[256,1536]{1,0:T(8,128)(2,1)}, u32[]{:S(2)}, u32[]{:S(2)}) collective-permute-start(bf16[256,1536]{1,0:T(8,128)(2,1)} %collective-permute-done.2), channel_id=1, source_target_pairs={{0,4},{4,8},{8,12},{12,16},{16,20},{20,24},{24,28},{28,0},{1,5},{5... | collective-permute-start | bytes 2359304 | tf_op jit(solution)/shard_map/ppermute | solution.py:22
  319.2 36.4 %collective-permute-start.5 = (bf16[256,1536]{1,0:T(8,128)(2,1)}, bf16[256,1536]{1,0:T(8,128)(2,1)S(1)}, u32[]{:S(2)}, u32[]{:S(2)}) collective-permute-start(bf16[256,1536]{1,0:T(8,128)(2,1)} %collective-permute-done.3), channel_id=1, source_target_pairs={{0,28},{4,0},{8,4},{12,8},{16,12},{20,16},{24,20},{28,24},{1,29},{... | collective-permute-start | bytes 2359304 | tf_op jit(solution)/shard_map/ppermute | solution.py:25
  346.7 19.8 %collective-permute-start.6 = (bf16[256,1536]{1,0:T(8,128)(2,1)}, bf16[256,1536]{1,0:T(8,128)(2,1)S(1)}, u32[]{:S(2)}, u32[]{:S(2)}) collective-permute-start(bf16[256,1536]{1,0:T(8,128)(2,1)} %collective-permute-done.4), channel_id=1, source_target_pairs={{0,4},{4,8},{8,12},{12,16},{16,20},{20,24},{24,28},{28,0},{1,5},{5... | collective-permute-start | bytes 2359304 | tf_op jit(solution)/shard_map/ppermute | solution.py:22
  673.0 318.6 %reduce-scatter.18.cloned.1.call-start = ((), (), s32[]{:S(2)}) async-start(), calls=%async_computation.23 | async-start | bytes 1179648 | tf_op jit(solution)/shard_map/reduce_scatter | solution.py:239
  872.0 131.5 %reduce-scatter.16.cloned.1.call-start = ((), (), s32[]{:S(2)}) async-start(), calls=%async_computation.22 | async-start | bytes 1179648 | tf_op jit(solution)/shard_map/reduce_scatter | solution.py:236
  888.0 161.5 %reduce-scatter.10.cloned.1.call-start = ((), (), s32[]{:S(2)}) async-start(), calls=%async_computation.17 | async-start | bytes 5242880 | tf_op jit(solution)/shard_map/reduce_scatter | solution.py:154
  899.0 222.8 %reduce-scatter.20.cloned.1.call-start = ((), (), s32[]{:S(2)}) async-start(), calls=%async_computation.24 | async-start | bytes 2359296 | tf_op jit(solution)/shard_map/reduce_scatter | solution.py:242
  907.4 285.8 %reduce-scatter.14.cloned.1.call-start = ((), (), s32[]{:S(2)}) async-start(), calls=%async_computation.21 | async-start | bytes 2359296 | tf_op jit(solution)/shard_map/reduce_scatter | solution.py:233
  948.0 291.0 %reduce-scatter.12.cloned.1.call-start = ((), (), s32[]{:S(2)}) async-start(), calls=%async_computation.20 | async-start | bytes 5242880 | tf_op jit(solution)/shard_map/reduce_scatter | solution.py:229
  955.8 404.7 %reduce-scatter.22.cloned.1.call-start = ((), (), s32[]{:S(2)}) async-start(), calls=%async_computation.25 | async-start | bytes 7077888 | tf_op jit(solution)/shard_map/reduce_scatter | solution.py:181
  967.4 513.9 %reduce-scatter.24.cloned.1.call-start = ((), (), s32[]{:S(2)}) async-start(), calls=%async_computation.26 | async-start | bytes 7077888 | tf_op jit(solution)/shard_map/reduce_scatter | solution.py:184
  979.2 624.4 %reduce-scatter.26.cloned.1.call-start = ((), (), s32[]{:S(2)}) async-start(), calls=%async_computation.27 | async-start | bytes 7077888 | tf_op jit(solution)/shard_map/reduce_scatter | solution.py:187
  990.6 248.5 %copy-start.9 = (bf16[1024,512]{1,0:T(8,128)(2,1)S(1)}, bf16[1024,512]{1,0:T(8,128)(2,1)}, u32[]{:S(2)}) copy-start(bf16[1024,512]{1,0:T(8,128)(2,1)} %param.13) | copy-start | bytes 3145732
  990.6 248.4 %copy-start.50 = (f32[1024]{0:T(1024)S(1)}, f32[1024]{0:T(1024)}, u32[]{:S(2)}) copy-start(f32[1024]{0:T(1024)} %copy-done.49) | copy-start | bytes 12292
  1195.1 410.9 %copy-start.52 = (f32[1024]{0:T(1024)S(1)}, f32[1024]{0:T(1024)}, u32[]{:S(2)}) copy-start(f32[1024]{0:T(1024)} %get-tuple-element.48) | copy-start | bytes 12292
  1239.0 366.9 %copy-start.26 = (bf16[1024,512]{1,0:T(8,128)(2,1)S(1)}, bf16[1024,512]{1,0:T(8,128)(2,1)}, u32[]{:S(2)}) copy-start(bf16[1024,512]{1,0:T(8,128)(2,1)} %reduce-scatter.12.cloned.1.call-done) | copy-start | bytes 3145732
  (56 other events, 339.2 us)
Sparse Core Ops, SparseCore 0:
  9.6 37.1 all-gather.8
  48.9 49.0 all-gather.14
  100.1 38.7 all-gather.12
  141.0 38.9 all-gather.10
  181.9 49.0 all-gather.16
  238.7 151.0 all-reduce.3
  392.0 98.8 all-gather.18
  492.4 32.6 all-gather.22
  527.1 99.4 all-gather.20
  673.1 151.0 all-reduce.5
  872.1 64.3 reduce-scatter.17
  940.4 63.1 reduce-scatter.15
  1006.0 43.4 reduce-scatter.9
  1052.9 68.9 reduce-scatter.19
  1125.8 67.3 reduce-scatter.13
  1195.6 43.3 reduce-scatter.11
  1242.5 117.9 reduce-scatter.21
  1363.9 117.2 reduce-scatter.23
  1484.8 118.7 reduce-scatter.25
